TPU v7x, 32 devices: a whole 2x2x4 slice. The times are simulated.
32 devices in a mesh: tm: 8 (over y, x, core), vocab: 4 (over z).
Axes of the slice: x: 2, y: 2, z: 4, core: 2. Of those that a mesh axis runs over, the one named last changes fastest.
Arguments:
- drift_noise: bfloat16 [64, 128, 8192], P('tm', None, 'vocab'), may hold values from -6 to 6
- counts: bfloat16 [64, 128, 8192], P('tm', None, 'vocab'), may hold values from 0 to 12, as said below
- base_logits: float32 [128, 8192], P(None, 'vocab'), may hold values from -8 to 300
- drift_scale: float32 [128], replicated, may hold values from 0.05 to 0.5
Outputs:
- grad_noise: bfloat16 [64, 128, 8192], P('tm', None, 'vocab')
- grad_base: float32 [128, 8192], P('tm', 'vocab')
Inputs may be any that keep to these rules, and one draw needn't show every extreme that they name: `counts`: whole numbers.
All inputs are finite; a program needn't handle non-finite values.
Results may differ from a plain program's by a relative error of at most 0.003.
Values sent between devices are 32-bit elements; how exact they have to be, the bound alone decides.
A program may use at most 128 MiB of HBM per device.

v0:
```python
import jax
import jax.numpy as jnp
from jax import lax
from jax.sharding import PartitionSpec as P


def entering(part, axis, combine, identity, reverse):
    count = lax.axis_size(axis)
    place = lax.axis_index(axis)
    ahead = count - 1 - place if reverse else place
    gathered = lax.all_gather(part, axis)
    state = jnp.zeros_like(part) + jnp.asarray(identity, part.dtype)

    def one(step, state):
        source = count - 1 - step if reverse else step
        return combine(state, lax.dynamic_index_in_dim(gathered, source, 0, False))

    return lax.fori_loop(0, ahead, one, state)


def from_root(block, axis, source):
    block = jnp.where(lax.axis_index(axis) == source, block, jnp.zeros_like(block))
    return lax.psum(block, axis)


def add_terms(earlier, later):
    return earlier + later


def per_device(drift_noise, counts, base_logits, drift_scale):
    spread = drift_scale[:, None]
    noise_f = drift_noise.astype(jnp.float32)
    local_drift = jnp.cumsum(spread[None] * noise_f, axis=0)
    blank = jnp.zeros(base_logits.shape, jnp.float32)
    before = entering(local_drift[-1], "tm", add_terms, blank, False)
    logits = base_logits[None] + before[None] + local_drift
    local_top = jnp.max(logits, axis=2)
    count_f = counts.astype(jnp.float32)
    local_tokens = jnp.sum(count_f, axis=2)
    top = lax.pmax(local_top, "vocab")
    expo = jnp.exp(logits - top[:, :, None])
    total, tokens = lax.psum((jnp.sum(expo, axis=2), local_tokens), "vocab")
    slope = count_f - tokens[:, :, None] * (expo / total[:, :, None])
    local_suffix = jnp.flip(jnp.cumsum(jnp.flip(slope, axis=0), axis=0), axis=0)
    block = local_suffix[0]
    later = entering(block, "tm", add_terms, blank, True)
    whole = from_root(later + block, "tm", 0)
    suffix = local_suffix + later[None]
    grad_noise = (spread[None] * suffix - noise_f).astype(jnp.bfloat16)
    topic_rows = whole.shape[0] // lax.axis_size("tm")
    row_start = lax.axis_index("tm") * topic_rows
    own_rows = lax.dynamic_slice_in_dim(whole, row_start, topic_rows, 0)
    return (grad_noise, own_rows)


def solution(mesh):
    return jax.shard_map(
        per_device,
        mesh=mesh,
        in_specs=(P("tm", None, "vocab"), P("tm", None, "vocab"), P(None, "vocab"), P()),
        out_specs=(P("tm", None, "vocab"), P("tm", "vocab")),
        check_vma=False,
    )
```

profile of v0, /device:TPU:1, one launch (start us, length us, event | category | flops | bytes accessed | tf_op | source)
XLA Modules:
  0.0 263.6 jit_solution(985525928569997044)
XLA Ops:
  7.2 3.0 %fusion = f32[8,128,2048]{2,1,0:T(8,128)S(1)} fusion(bf16[8,128,2048]{2,1,0:T(8,128)(2,1)} %param.8, f32[128]{0:T(128)} %param.11), kind=kOutput, calls=%fused_computation.6 | output fusion | flops 18874368 | bytes 12583424 | tf_op jit(solution)/shard_map/jit(cumsum)/reduce_window_sum | solution.py:33
  10.3 3.2 %copy-done = f32[8,128,2048]{2,1,0:T(8,128)} copy-done((f32[8,128,2048]{2,1,0:T(8,128)}, f32[8,128,2048]{2,1,0:T(8,128)S(1)}, u32[]{:S(2)}) %copy-start) | copy-done | bytes 8388632
  13.5 1.1 slice.9
  14.5 0.0 all-gather.5.cloned.1.call-start
  14.6 2.8 %convert_reduce_fusion = f32[8,128]{1,0:T(8,128)S(1)} fusion(bf16[8,128,2048]{2,1,0:T(8,128)(2,1)} %param.9), kind=kLoop, calls=%fused_computation.5 | loop fusion | flops 4193280 | bytes 4198400 | tf_op jit(solution)/shard_map/reduce_sum | solution.py:39
  17.4 54.0 %all-gather.3.cloned.1.call-done = f32[8,128,2048]{2,1,0:T(8,128)} async-done(((f32[1,128,2048]{2,1,0:T(8,128)}), f32[8,128,2048]{2,1,0:T(8,128)}) %all-gather.3.cloned.1.call-update) | async-done | bytes 8388624 | tf_op jit(solution)/shard_map/all_gather | solution.py:11
  71.4 0.1 broadcast.9.clone
  71.5 1.5 while.22
  71.6 1.5 bitcast_add_fusion.5
  73.1 0.1 add.61
  73.2 4.0 %add_reduce_fusion = f32[8,128]{1,0:T(8,128)S(1)} fusion(f32[8,128,2048]{2,1,0:T(8,128)} %copy-done, f32[128,2048]{1,0:T(8,128)S(1)} %add.61), kind=kLoop, calls=%fused_computation.9 | loop fusion | flops 4193280 | bytes 9441280 | tf_op jit(solution)/shard_map/reduce_max | solution.py:37
  77.2 9.7 %pmax.7 = f32[8,128]{1,0:T(8,128)S(1)} all-reduce(f32[8,128]{1,0:T(8,128)S(1)} %add_reduce_fusion), channel_id=1, replica_groups=mesh['tm'=8,'vocab'=4] {'vocab'}, use_global_device_ids=true, to_apply=%region_6.7 | all-reduce | flops 1024 | bytes 8192 | tf_op jit(solution)/shard_map/pmax | solution.py:40
  86.9 4.3 %fusion.2 = f32[8,128]{1,0:T(8,128)S(1)} fusion(f32[8,128,2048]{2,1,0:T(8,128)} %copy-done, f32[8,128]{1,0:T(8,128)S(1)} %pmax.7, f32[128,2048]{1,0:T(8,128)S(1)} %add.61), kind=kLoop, calls=%fused_computation.10 | loop fusion | flops 6290432 | bytes 9445376 | tf_op jit(solution)/shard_map/reduce_sum | solution.py:42
  91.2 6.8 %all-reduce = (f32[8,128]{1,0:T(8,128)S(1)}, f32[8,128]{1,0:T(8,128)S(1)}) all-reduce(f32[8,128]{1,0:T(8,128)S(1)} %fusion.2, f32[8,128]{1,0:T(8,128)S(1)} %convert_reduce_fusion), channel_id=1, replica_groups=mesh['tm'=8,'vocab'=4] {'vocab'}, use_global_device_ids=true, to_apply=%region_8.9 | all-reduce | flops 2048 | bytes 16384 | tf_op jit(solution)/shard_map/psum | solution.py:42
  98.0 8.2 %convert_subtract_fusion.1 = f32[8,128,2048]{2,1,0:T(8,128)} fusion(bf16[8,128,2048]{2,1,0:T(8,128)(2,1)} %param.9, f32[8,128,2048]{2,1,0:T(8,128)} %copy-done, f32[8,128]{1,0:T(8,128)S(1)} %get-tuple-element.99, f32[8,128]{1,0:T(8,128)S(1)} %pmax.7, f32[128,2048]{1,0:T(8,128)S(1)} %add.61, f32[8,128]{1,0:T(8,128)S(1)} %get-tuple-element.100), kind=kLoop, calls=%fused_computation.4 | loop fusion | flops 12582912 | bytes 22032384 | tf_op jit(solution)/shard_map/sub | solution.py:43
  106.2 7.7 %rev.7 = f32[8,128,2048]{2,1,0:T(8,128)} reverse(f32[8,128,2048]{2,1,0:T(8,128)} %convert_subtract_fusion.1), dimensions={0} | reverse | bytes 16777216 | tf_op jit(solution)/shard_map/jit(_flip)/rev | solution.py:44
  113.9 7.1 %fusion.5 = f32[8,128,2048]{2,1,0:T(8,128)} fusion(f32[8,128,2048]{2,1,0:T(8,128)} %rev.7), kind=kOutput, calls=%fused_computation.15 | output fusion | flops 14680064 | bytes 16777216 | tf_op jit(solution)/shard_map/jit(cumsum)/reduce_window_sum | solution.py:44
  121.0 2.3 slice.10
  123.4 0.0 all-reduce.3.cloned.1.call-start
  123.4 64.4 %all-gather.5.cloned.1.call-done = f32[8,128,2048]{2,1,0:T(8,128)} async-done(((f32[1,128,2048]{2,1,0:T(8,128)}), f32[8,128,2048]{2,1,0:T(8,128)}) %all-gather.5.cloned.1.call-update) | async-done | bytes 8388624 | tf_op jit(solution)/shard_map/all_gather | solution.py:11
  187.8 0.1 broadcast.9
  187.9 9.1 %while.23 = (s32[]{:T(128)}, f32[128,2048]{1,0:T(8,128)S(1)}, s32[]{:T(128)}, f32[8,128,2048]{2,1,0:T(8,128)}, s32[]{:T(128)}, /*index=5*/s32[]{:T(128)}, s32[]{:T(128)}, s32[]{:T(128)}) while((s32[]{:T(128)}, f32[128,2048]{1,0:T(8,128)S(1)}, s32[]{:T(128)}, f32[8,128,2048]{2,1,0:T(8,128)}, s32[]{:T(128)}, /*index=5*/s32[]{:T(128)}, ...), condition=%wide.region_11.12_spmd, body=%wide.region_10.11_spmd.sunk | while | flops 262150 | bytes 3145863 | solution.py:18
  187.9 1.5 bitcast_add_fusion.6
  189.4 1.5 bitcast_add_fusion.6
  190.9 1.5 bitcast_add_fusion.6
  192.5 1.5 bitcast_add_fusion.6
  194.0 1.5 bitcast_add_fusion.6
  195.5 1.5 bitcast_add_fusion.6
  197.0 2.3 fusion.4
  199.3 8.7 %fusion.1 = bf16[8,128,2048]{2,1,0:T(8,128)(2,1)} fusion(bf16[8,128,2048]{2,1,0:T(8,128)(2,1)} %param.8, f32[8,128,2048]{2,1,0:T(8,128)} %fusion.5, f32[128,2048]{1,0:T(8,128)S(1)} %get-tuple-element.82, f32[128]{0:T(128)S(1)} %copy-done.2), kind=kLoop, calls=%fused_computation.7 | loop fusion | flops 10485760 | bytes 17826304 | tf_op jit(solution)/shard_map/convert_element_type | solution.py:49
  208.1 47.5 %all-reduce.3.cloned.1.call-done = f32[128,2048]{1,0:T(8,128)} async-done(((f32[128,2048]{1,0:T(8,128)}), f32[128,2048]{1,0:T(8,128)}) %all-reduce.3.cloned.1.call-update) | async-done | bytes 1048592 | tf_op jit(solution)/shard_map/psum | solution.py:23
  255.5 1.6 constant_dynamic-slice_fusion
  (9 shorter events, 0.1 us)
Async XLA Ops:
  7.2 64.3 %all-gather.3.cloned.1.call-start = ((), (), s32[]{:S(2)}) async-start(), calls=%async_computation | async-start | bytes 9437184 | tf_op jit(solution)/shard_map/all_gather | solution.py:11
  10.3 3.2 %copy-start = (f32[8,128,2048]{2,1,0:T(8,128)}, f32[8,128,2048]{2,1,0:T(8,128)S(1)}, u32[]{:S(2)}) copy-start(f32[8,128,2048]{2,1,0:T(8,128)S(1)} %fusion) | copy-start | bytes 25165828
  14.5 173.2 %all-gather.5.cloned.1.call-start = ((), (), s32[]{:S(2)}) async-start(), calls=%async_computation.1 | async-start | bytes 9437184 | tf_op jit(solution)/shard_map/all_gather | solution.py:11
  17.4 55.7 %copy-start.1 = (f32[128,2048]{1,0:T(8,128)S(1)}, f32[128,2048]{1,0:T(8,128)}, u32[]{:S(2)}) copy-start(f32[128,2048]{1,0:T(8,128)} %param.10) | copy-start | bytes 3145732
  123.4 132.2 %all-reduce.3.cloned.1.call-start = ((), (), s32[]{:S(2)}) async-start(), calls=%async_computation.2 | async-start | bytes 2097152 | tf_op jit(solution)/shard_map/psum | solution.py:23
  187.9 11.5 %copy-start.2 = (f32[128]{0:T(128)S(1)}, f32[128]{0:T(128)}, u32[]{:S(2)}) copy-start(f32[128]{0:T(128)} %param.11) | copy-start | bytes 1540
Sparse Core Ops, SparseCore 0:
  14.7 56.7 all-gather.2
  123.5 64.2 all-gather.4
  199.5 56.0 all-reduce.2
where the time goes:
time: 266 us; the launch traced here: 264 us
  waiting for transfers between devices  166 us (62%)
  other arithmetic  51 us (19%)
  blocking collectives  16.5 us (6%)
  local copies, waits for them, and re-layouts  16 us (6%)
  between operations  13.9 us (5%)
    all_gather x2, waiting for transfers between devices, entering(): gathered = lax.all_gather(part, axis)  118 us
    psum x1, waiting for transfers between devices, from_root(): return lax.psum(block, axis)  47.5 us
    add x7, other arithmetic, add_terms(): return earlier + later  10.4 us
    pmax x1, blocking collectives, per_device(): top = lax.pmax(local_top, 'vocab')  9.68 us
    convert_element_type x1, other arithmetic, per_device(): grad_noise = (spread[None] * suffix - noise_f).astype(jnp.bfloat16)  8.71 us
    sub x1, other arithmetic, per_device(): slope = count_f - tokens[:, :, None] * (expo / total[:, :, None])  8.19 us
    rev x1, local copies, waits for them, and re-layouts, per_device(): local_suffix = jnp.flip(jnp.cumsum(jnp.flip(slope, axis=0), axis=0), axis=0)  7.71 us
    another operation x1, other arithmetic, per_device(): local_suffix = jnp.flip(jnp.cumsum(jnp.flip(slope, axis=0), axis=0), axis=0)  7.14 us
  transfers between devices with their start and end apart: 3, of which 3 were waited for; matrix products, arithmetic and copies ran while one was open for 4% of the time, Pallas kernels for 0%

commit v1 on v0

v1 whole, which is shorter than its diff:
```python
import functools

import jax
import jax.numpy as jnp
from jax import lax
from jax.experimental import pallas as pl
from jax.experimental.pallas import tpu as pltpu
from jax.sharding import PartitionSpec as P

MESH = pl.DeviceIdType.MESH
KC = 16
HB = KC // 2
LANE = 128


def kernel(n, nz, nb, rows, out_rows, dims,
           noise_hbm, counts_hbm, base_hbm, scale_ref, gn_hbm, gb_hbm,
           noise, counts, base, spread, work, out, query, ratio, stat, stat_in, tot, tot_out,
           own, mate, src, got, acc,
           in_sem, out_sem, gb_sem, mate_s, mate_r, hop_s, hop_r, acc_s, acc_r, stat_s, stat_r, tot_s, tot_r):
    T, K, V = dims
    NC = K // KC
    LB = min(256, V)
    me = lax.axis_index("tm")
    z = lax.axis_index("vocab")
    core = lax.rem(me, 2)
    partner = me + 1 - 2 * core

    def bit(j):
        return lax.rem(me // (2 ** j), 2)

    def across(j):
        return me + (1 - 2 * bit(j)) * (2 ** j)

    def krows(c):
        return pl.ds(pl.multiple_of(c * KC, KC), KC)

    def load_noise(c):
        return pltpu.make_async_copy(noise_hbm.at[:, krows(c), :], noise.at[c], in_sem.at[0, c])

    def load_counts(c):
        return pltpu.make_async_copy(counts_hbm.at[:, krows(c), :], counts.at[c], in_sem.at[1, c])

    def load_base(c):
        return pltpu.make_async_copy(base_hbm.at[krows(c), :], base.at[c], in_sem.at[2, c])

    def store_out(c):
        return pltpu.make_async_copy(out.at[c], gn_hbm.at[:, krows(c), :], out_sem.at[c])

    def send(a, b, s, r, device):
        return pltpu.make_async_remote_copy(src_ref=a, dst_ref=b, send_sem=s, recv_sem=r,
                                            device_id=device, device_id_type=MESH)

    def mate_copy(p, c):
        return send(own.at[p, c], mate.at[p, c], mate_s.at[p, c], mate_r.at[p, c], {"tm": partner})

    def hop_copy(p, j, c):
        return send(src.at[p, j, c], got.at[p, j, c], hop_s.at[p, j, c], hop_r.at[p, j, c],
                    {"tm": across(j + 1)})

    def acc_copy(p, c):
        return send(acc.at[p, c, core], acc.at[p, c, core], acc_s.at[p, c], acc_r.at[p, c], {"tm": partner})

    def stat_copy(d, c):
        return send(stat.at[c], stat_in.at[d - 1, c], stat_s.at[d - 1, c], stat_r.at[d - 1, c],
                    {"vocab": lax.rem(z + d, nz)})

    def tot_copy():
        return send(tot_out, tot.at[core], tot_s.at[0], tot_r.at[0], {"tm": partner})

    def start_loads(c, _):
        load_noise(c).start()
        load_base(c).start()
        return 0

    lax.fori_loop(0, NC, start_loads, 0)
    lax.fori_loop(0, NC, lambda c, _: (load_counts(c).start(), 0)[1], 0)

    barrier = pltpu.get_barrier_semaphore()
    for j in range(nb + 1):
        pl.semaphore_signal(barrier, inc=1, device_id={"tm": across(j)}, device_id_type=MESH)
    for d in range(1, nz):
        pl.semaphore_signal(barrier, inc=1, device_id={"vocab": lax.rem(z + d, nz)}, device_id_type=MESH)
    pl.semaphore_wait(barrier, nb + nz)

    wide = jnp.broadcast_to(scale_ref[...], (LANE, LANE)).T
    for c in range(NC):
        spread[c] = wide[c * KC:(c + 1) * KC]

    def lanes(i):
        return pl.ds(pl.multiple_of(i * LB, LB), LB)

    def tiled(x):
        return jnp.concatenate([x] * (LB // LANE), axis=1)

    def two(x):
        return x.reshape(2, HB, x.shape[-1])

    def drift(c):
        load_noise(c).wait()
        sp = tiled(spread[c])

        def block(i, _):
            total = jnp.zeros((KC, LB), jnp.float32)
            for t in range(T):
                total = total + sp * noise[c, t, :, lanes(i)].astype(jnp.float32)
                work[c, t, :, lanes(i)] = total
            own[0, c, :, :, lanes(i)] = two(total)
            return 0

        lax.fori_loop(0, V // LB, block, 0)
        mate_copy(0, c).start()

    def first_hop(p, c):
        mate_copy(p, c).wait_recv()
        src[p, 0, c] = own[p, c, core] + mate[p, c, core]
        hop_copy(p, 0, c).start()

    def next_hop(p, j, c):
        hop_copy(p, j, c).wait_recv()
        arrived = got[p, j, c]
        wanted = bit(j + 1) == (1 - p)
        before = jnp.where(wanted, arrived, jnp.zeros_like(arrived))
        if j > 0:
            before = before + acc[p, c, core]
        acc[p, c, core] = before
        if j < nb - 1:
            src[p, j + 1, c] = src[p, j, c] + arrived
            hop_copy(p, j + 1, c).start()
            return
        acc_copy(p, c).start()
        if p == 1:
            @pl.when((me * rows) // KC == c)
            def _():
                tot[core] = src[p, j, c] + arrived

            @pl.when((partner * rows) // KC == c)
            def _():
                tot_out[...] = src[p, j, c] + arrived
                tot_copy().start()

    def entering(p, c, i):
        x = acc[p, c, :, :, lanes(i)].reshape(KC, LB)
        m = mate[p, c, :, :, lanes(i)].reshape(KC, LB)
        return x + jnp.where(core == 1 - p, m, jnp.zeros_like(m))

    def soft(c):
        acc_copy(0, c).wait_recv()
        load_base(c).wait()

        def seek(i, top):
            q = base[c, :, lanes(i)] + entering(0, c, i)
            query[:, lanes(i)] = q
            for b in range(LB // LANE):
                top = jnp.maximum(top, q[:, b * LANE:(b + 1) * LANE])
            return top

        top = lax.fori_loop(0, V // LB, seek, jnp.full((KC, LANE), -jnp.inf, jnp.float32))
        top = jnp.broadcast_to(jnp.max(top, axis=1, keepdims=True), (KC, LANE))
        tops = tiled(top)

        def block(i, sums):
            q = query[:, lanes(i)] - tops
            new = []
            for t in range(T):
                e = jnp.exp(work[c, t, :, lanes(i)] + q)
                work[c, t, :, lanes(i)] = e
                s = sums[t]
                for b in range(LB // LANE):
                    s = s + e[:, b * LANE:(b + 1) * LANE]
                new.append(s)
            return tuple(new)

        sums = lax.fori_loop(0, V // LB, block, tuple(jnp.zeros((KC, LANE), jnp.float32) for _ in range(T)))
        load_counts(c).wait()
        tokens = jnp.dot(counts[c].reshape(T * KC, V), jnp.ones((V, LANE), jnp.bfloat16),
                         preferred_element_type=jnp.float32)
        lane = lax.broadcasted_iota(jnp.int32, (KC, LANE), 1)
        packed = jnp.zeros((KC, LANE), jnp.float32)
        for t in range(T):
            s = jnp.broadcast_to(jnp.sum(sums[t], axis=1, keepdims=True), (KC, LANE))
            packed = jnp.where(lane == t, s, packed)
            packed = jnp.where(lane == T + t, tokens[t * KC:(t + 1) * KC], packed)
        stat[c, 0] = packed
        stat[c, 1] = top
        for d in range(1, nz):
            stat_copy(d, c).start()

    def slopes(c):
        for d in range(1, nz):
            stat_copy(d, c).wait_recv()
        mine, top = stat[c, 0], stat[c, 1]
        best = top
        for d in range(1, nz):
            best = jnp.maximum(best, stat_in[d - 1, c, 1])
        factor = jnp.exp(top - best)
        total = mine * factor
        tokens = mine
        for d in range(1, nz):
            total = total + stat_in[d - 1, c, 0] * jnp.exp(stat_in[d - 1, c, 1] - best)
            tokens = tokens + stat_in[d - 1, c, 0]
        r = factor * pltpu.roll(tokens, LANE - T, 1) / total
        for t in range(T):
            ratio[t] = jnp.broadcast_to(r[:, t:t + 1], (KC, LANE))
        sp = tiled(spread[c])

        def block(i, _):
            run = jnp.zeros((KC, LB), jnp.float32)
            for t in reversed(range(T)):
                run = run + (counts[c, t, :, lanes(i)].astype(jnp.float32)
                             - tiled(ratio[t]) * work[c, t, :, lanes(i)])
                work[c, t, :, lanes(i)] = sp * run - noise[c, t, :, lanes(i)].astype(jnp.float32)
            own[1, c, :, :, lanes(i)] = two(run)
            return 0

        lax.fori_loop(0, V // LB, block, 0)
        mate_copy(1, c).start()

    def finish(c):
        acc_copy(1, c).wait_recv()
        sp = tiled(spread[c])

        def block(i, _):
            later = sp * entering(1, c, i)
            for t in range(T):
                out[c, t, :, lanes(i)] = (work[c, t, :, lanes(i)] + later).astype(jnp.bfloat16)
            return 0

        lax.fori_loop(0, V // LB, block, 0)
        store_out(c).start()

    span = nb + 3
    forward = []
    for p in (0, 1):
        for j in reversed(range(nb)):
            forward.append((p * span + 2 + j, functools.partial(next_hop, p, j)))
        forward.append((p * span + 1, functools.partial(first_hop, p)))
    heavy = [(span, slopes), (nb + 2, soft), (0, drift), (span + nb + 2, finish)]

    def tick(s, _):
        for off, stage in forward + heavy:
            @pl.when((s >= off) & (s < off + NC))
            def _():
                stage(s - off)
        return 0

    lax.fori_loop(0, NC + span + nb + 2 + 1, tick, 0)


    tot_copy().wait()
    first = me * rows - ((me * rows) // KC) * KC
    if out_rows == KC:
        done = [pltpu.make_async_copy(tot.at[h], gb_hbm.at[pl.ds(h * HB, HB), :], gb_sem.at[h]) for h in range(2)]
    else:
        done = [pltpu.make_async_copy(tot.at[first // HB], gb_hbm, gb_sem.at[0])]
    for copy in done:
        copy.start()

    def drain(c, _):
        for p in (0, 1):
            mate_copy(p, c).wait_send()
            for j in range(nb):
                hop_copy(p, j, c).wait_send()
            acc_copy(p, c).wait_send()
        for d in range(1, nz):
            stat_copy(d, c).wait_send()
        store_out(c).wait()
        return 0

    lax.fori_loop(0, NC, drain, 0)
    for copy in done:
        copy.wait()


def per_device(n, nz, drift_noise, counts, base_logits, drift_scale):
    T, K, V = drift_noise.shape
    nb = n.bit_length() - 2
    rows = K // n
    out_rows = KC if rows >= KC else HB
    NC = K // KC
    f32, bf16 = jnp.float32, jnp.bfloat16
    dma = pltpu.SemaphoreType.DMA
    any_space = pl.BlockSpec(memory_space=pl.ANY)
    peers = max(nz - 1, 1)
    grad_noise, grad_base = pl.pallas_call(
        functools.partial(kernel, n, nz, nb, rows, out_rows, (T, K, V)),
        out_shape=(jax.ShapeDtypeStruct((T, K, V), bf16), jax.ShapeDtypeStruct((out_rows, V), f32)),
        in_specs=[any_space, any_space, any_space, pl.BlockSpec(memory_space=pltpu.VMEM)],
        out_specs=(any_space, any_space),
        scratch_shapes=[
            pltpu.VMEM((NC, T, KC, V), bf16),
            pltpu.VMEM((NC, T, KC, V), bf16),
            pltpu.VMEM((NC, KC, V), f32),
            pltpu.VMEM((NC, KC, LANE), f32),
            pltpu.VMEM((NC, T, KC, V), f32),
            pltpu.VMEM((NC, T, KC, V), bf16),
            pltpu.VMEM((KC, V), f32),
            pltpu.VMEM((T, KC, LANE), f32),
            pltpu.VMEM((NC, 2, KC, LANE), f32),
            pltpu.VMEM((peers, NC, 2, KC, LANE), f32),
            pltpu.VMEM((2, HB, V), f32),
            pltpu.VMEM((HB, V), f32),
            pltpu.VMEM((2, NC, 2, HB, V), f32),
            pltpu.VMEM((2, NC, 2, HB, V), f32),
            pltpu.VMEM((2, nb, NC, HB, V), f32),
            pltpu.VMEM((2, nb, NC, HB, V), f32),
            pltpu.VMEM((2, NC, 2, HB, V), f32),
            dma((3, NC)), dma((NC,)), dma((2,)),
            dma((2, NC)), dma((2, NC)),
            dma((2, nb, NC)), dma((2, nb, NC)),
            dma((2, NC)), dma((2, NC)),
            dma((peers, NC)), dma((peers, NC)),
            dma((1,)), dma((1,)),
        ],
        compiler_params=pltpu.CompilerParams(
            collective_id=0, has_side_effects=True, vmem_limit_bytes=60 * 1024 * 1024),
    )(drift_noise, counts, base_logits, drift_scale.reshape(1, K))
    if rows < out_rows:
        start = lax.rem(lax.axis_index("tm") * rows, out_rows)
        grad_base = lax.dynamic_slice_in_dim(grad_base, start, rows, 0)
    return grad_noise, grad_base


def solution(mesh):
    n, nz = mesh.shape["tm"], mesh.shape["vocab"]
    return jax.shard_map(
        functools.partial(per_device, n, nz),
        mesh=mesh,
        in_specs=(P("tm", None, "vocab"), P("tm", None, "vocab"), P(None, "vocab"), P()),
        out_specs=(P("tm", None, "vocab"), P("tm", "vocab")),
        check_vma=False,
    )
```

time: 266 us -> 74.5 us (0.28)
  waiting for transfers between devices: 166 us -> 0 us
  Pallas kernels: 0 us -> 68.2 us
  other arithmetic: 51 us -> 0 us
  blocking collectives: 16.5 us -> 0 us
  between operations: 13.9 us -> 0.65 us
  local copies, waits for them, and re-layouts: 16 us -> 5.48 us
    all_gather x2 -> x0, waiting for transfers between devices: 118 us -> none  [entering(): gathered = lax.all_gather(part, axis)]
    pallas_call x0 -> x1, Pallas kernels: none -> 68.2 us  [per_device(): pl.pallas_call(functools.partial(kernel, n, nz, nb, rows, out_rows, (T, K...]
    psum x1 -> x0, waiting for transfers between devices: 47.5 us -> none  [from_root(): return lax.psum(block, axis)]
    add x8 -> x0, other arithmetic: 10.5 us -> none  [the longest x7 10.4 us: add_terms(): return earlier + later]
    another operation x2 -> x0, other arithmetic: 10.2 us -> none  [the longest x1 7.14 us: per_device(): local_suffix = jnp.flip(jnp.cumsum(jnp.flip(slope, axis=0), axis=0), axis=0)]
    pmax x1 -> x0, blocking collectives: 9.68 us -> none  [per_device(): top = lax.pmax(local_top, 'vocab')]
    convert_element_type x1 -> x0, other arithmetic: 8.71 us -> none  [per_device(): grad_noise = (spread[None] * suffix - noise_f).astype(jnp.bfloat16)]
    sub x1 -> x0, other arithmetic: 8.19 us -> none  [per_device(): slope = count_f - tokens[:, :, None] * (expo / total[:, :, None])]
  transfers between devices with their start and end apart: 3 -> 0, of which waited for: 3 -> 0; matrix products, arithmetic and copies ran while one was open for 4% -> 0% of each run, Pallas kernels for 0% -> 0%
where the time goes in v1:
time: 74.5 us; the launch traced here: 74.3 us
  Pallas kernels  68.2 us (92%)
  local copies, waits for them, and re-layouts  5.48 us (7%)
    pallas_call x1, Pallas kernels, per_device(): pl.pallas_call(functools.partial(kernel, n, nz, nb, rows, out_rows, (T, K...  68.2 us
    unnamed x4, local copies, waits for them, and re-layouts  5.48 us

profile of v1, /device:TPU:1, one launch (start us, length us, event | category | flops | bytes accessed | tf_op | source)
XLA Modules:
  0.0 74.3 jit_solution(5277728722740480188)
XLA Ops:
  0.6 68.2 %shard_map.59 = (bf16[8,128,2048]{2,1,0:T(8,128)(2,1)}, f32[16,2048]{1,0:T(8,128)}) custom-call(bf16[8,128,2048]{2,1,0:T(8,128)(2,1)} %noise_hbm.1, bf16[8,128,2048]{2,1,0:T(8,128)(2,1)} %counts_hbm.1, f32[128,2048]{1,0:T(8,128)} %base_hbm.1, f32[1,128]{1,0:T(1,128)} %bitcast.1), custom_call_target="tpu_custom_call" | custom-call | tf_op jit(solution)/shard_map/pallas_call | solution.py:285
  68.8 0.0 copy-start
  68.8 4.8 %copy.8 = bf16[8,128,2048]{2,1,0:T(8,128)(2,1)} copy(bf16[8,128,2048]{2,1,0:T(8,128)(2,1)} %get-tuple-element.4) | data formatting | bytes 8388608
  73.7 0.0 copy-done
  73.7 0.7 copy.9
Async XLA Ops:
  68.8 4.8 %copy-start = (f32[16,2048]{1,0:T(8,128)S(1)}, f32[16,2048]{1,0:T(8,128)}, u32[]{:S(2)}) copy-start(f32[16,2048]{1,0:T(8,128)} %get-tuple-element.5) | copy-start | bytes 393220

commit v2 on v1

--- a/solution.py
+++ b/solution.py
@@ -11,13 +11,14 @@
 KC = 16
 HB = KC // 2
 LANE = 128
+GAP = (1, 3, 3)
 
 
 def kernel(n, nz, nb, rows, out_rows, dims,
-           noise_hbm, counts_hbm, base_hbm, scale_ref, gn_hbm, gb_hbm,
-           noise, counts, base, spread, work, out, query, ratio, stat, stat_in, tot, tot_out,
+           noise_hbm, counts_hbm, base_hbm, scale_hbm, gn_hbm, gb_hbm,
+           noise, counts, base, scale_ref, spread, work, out, query, ratio, stat, stat_in, tot, tot_out,
            own, mate, src, got, acc,
-           in_sem, out_sem, gb_sem, mate_s, mate_r, hop_s, hop_r, acc_s, acc_r, stat_s, stat_r, tot_s, tot_r):
+           in_sem, out_sem, gb_sem, scale_sem, mate_s, mate_r, hop_s, hop_r, acc_s, acc_r, stat_s, stat_r, tot_s, tot_r):
     T, K, V = dims
     NC = K // KC
     LB = min(256, V)
@@ -73,6 +74,8 @@
         load_base(c).start()
         return 0
 
+    load_scale = pltpu.make_async_copy(scale_hbm, scale_ref, scale_sem.at[0])
+    load_scale.start()
     lax.fori_loop(0, NC, start_loads, 0)
     lax.fori_loop(0, NC, lambda c, _: (load_counts(c).start(), 0)[1], 0)
 
@@ -83,6 +86,7 @@
         pl.semaphore_signal(barrier, inc=1, device_id={"vocab": lax.rem(z + d, nz)}, device_id_type=MESH)
     pl.semaphore_wait(barrier, nb + nz)
 
+    load_scale.wait()
     wide = jnp.broadcast_to(scale_ref[...], (LANE, LANE)).T
     for c in range(NC):
         spread[c] = wide[c * KC:(c + 1) * KC]
@@ -229,13 +233,22 @@
         lax.fori_loop(0, V // LB, block, 0)
         store_out(c).start()
 
-    span = nb + 3
-    forward = []
+    gap = GAP
+    at, plan = 0, []
     for p in (0, 1):
-        for j in reversed(range(nb)):
-            forward.append((p * span + 2 + j, functools.partial(next_hop, p, j)))
-        forward.append((p * span + 1, functools.partial(first_hop, p)))
-    heavy = [(span, slopes), (nb + 2, soft), (0, drift), (span + nb + 2, finish)]
+        at += gap[0]
+        stages = [(at, functools.partial(first_hop, p))]
+        for j in range(nb):
+            at += gap[1]
+            stages.append((at, functools.partial(next_hop, p, j)))
+        at += gap[0]
+        plan = stages[::-1] + plan
+        if p == 0:
+            enter = at
+            at += gap[2]
+            leave = at
+    heavy = [(leave, slopes), (enter, soft), (0, drift), (at, finish)]
+    forward = plan
 
     def tick(s, _):
         for off, stage in forward + heavy:
@@ -244,7 +257,7 @@
                 stage(s - off)
         return 0
 
-    lax.fori_loop(0, NC + span + nb + 2 + 1, tick, 0)
+    lax.fori_loop(0, NC + at, tick, 0)
 
 
     tot_copy().wait()
@@ -285,12 +298,13 @@
     grad_noise, grad_base = pl.pallas_call(
         functools.partial(kernel, n, nz, nb, rows, out_rows, (T, K, V)),
         out_shape=(jax.ShapeDtypeStruct((T, K, V), bf16), jax.ShapeDtypeStruct((out_rows, V), f32)),
-        in_specs=[any_space, any_space, any_space, pl.BlockSpec(memory_space=pltpu.VMEM)],
+        in_specs=[any_space] * 4,
         out_specs=(any_space, any_space),
         scratch_shapes=[
             pltpu.VMEM((NC, T, KC, V), bf16),
             pltpu.VMEM((NC, T, KC, V), bf16),
             pltpu.VMEM((NC, KC, V), f32),
+            pltpu.VMEM((1, K), f32),
             pltpu.VMEM((NC, KC, LANE), f32),
             pltpu.VMEM((NC, T, KC, V), f32),
             pltpu.VMEM((NC, T, KC, V), bf16),
@@ -305,7 +319,7 @@
             pltpu.VMEM((2, nb, NC, HB, V), f32),
             pltpu.VMEM((2, nb, NC, HB, V), f32),
             pltpu.VMEM((2, NC, 2, HB, V), f32),
-            dma((3, NC)), dma((NC,)), dma((2,)),
+            dma((3, NC)), dma((NC,)), dma((2,)), dma((1,)),
             dma((2, NC)), dma((2, NC)),
             dma((2, nb, NC)), dma((2, nb, NC)),
             dma((2, NC)), dma((2, NC)),
@@ -313,8 +327,8 @@
             dma((1,)), dma((1,)),
         ],
         compiler_params=pltpu.CompilerParams(
-            collective_id=0, has_side_effects=True, vmem_limit_bytes=60 * 1024 * 1024),
-    )(drift_noise, counts, base_logits, drift_scale.reshape(1, K))
+            collective_id=0, has_side_effects=True, vmem_limit_bytes=40 * 1024 * 1024),
+    )(*[pltpu.with_memory_space_constraint(x, pltpu.HBM) for x in (drift_noise, counts, base_logits, drift_scale.reshape(1, K))])
     if rows < out_rows:
         start = lax.rem(lax.axis_index("tm") * rows, out_rows)
         grad_base = lax.dynamic_slice_in_dim(grad_base, start, rows, 0)

time: 74.5 us -> 48.1 us (0.65)
  Pallas kernels: 68.2 us -> 44.6 us
  local copies, waits for them, and re-layouts: 5.48 us -> 2.67 us
    pallas_call x1, Pallas kernels: 68.2 us -> 44.6 us  [per_device(): pl.pallas_call(functools.partial(kernel, n, nz, nb, rows, out_rows, (T, K...]
    unnamed x4 -> x2, local copies, waits for them, and re-layouts: 5.48 us -> 2.67 us
where the time goes in v2:
time: 48.1 us; the launch traced here: 47.9 us
  Pallas kernels  44.6 us (93%)
  local copies, waits for them, and re-layouts  2.67 us (6%)
  between operations  0.64 us (1%)
    pallas_call x1, Pallas kernels, per_device(): pl.pallas_call(functools.partial(kernel, n, nz, nb, rows, out_rows, (T, K...  44.6 us
    unnamed x2, local copies, waits for them, and re-layouts  2.67 us

profile of v2, /device:TPU:1, one launch (start us, length us, event | category | flops | bytes accessed | tf_op | source)
XLA Modules:
  0.0 47.9 jit_solution(1216283094344296210)
XLA Ops:
  0.6 44.6 %shard_map.59 = (bf16[8,128,2048]{2,1,0:T(8,128)(2,1)S(1)}, f32[16,2048]{1,0:T(8,128)S(1)}) custom-call(bf16[8,128,2048]{2,1,0:T(8,128)(2,1)} %noise_hbm.1, bf16[8,128,2048]{2,1,0:T(8,128)(2,1)} %counts_hbm.1, f32[128,2048]{1,0:T(8,128)} %base_hbm.1, f32[1,128]{1,0:T(1,128)} %bitcast.1), custom_call_target="tpu_custom_call" | custom-call | tf_op jit(solution)/shard_map/pallas_call | solution.py:298
  45.3 2.0 %copy.8 = bf16[8,128,2048]{2,1,0:T(8,128)(2,1)} copy(bf16[8,128,2048]{2,1,0:T(8,128)(2,1)S(1)} %get-tuple-element.4) | data formatting | bytes 8388608
  47.3 0.7 %copy.9 = f32[16,2048]{1,0:T(8,128)} copy(f32[16,2048]{1,0:T(8,128)S(1)} %get-tuple-element.5) | data formatting | bytes 262144
